TPU v7x, 512 devices: a whole 4x8x8 slice. The times are simulated.
512 devices in a mesh: dp: 4 (over x), expert: 16 (over z, core), etp: 8 (over y).
Axes of the slice: x: 4, y: 8, z: 8, core: 2. Of those that a mesh axis runs over, the one named last changes fastest.
Arguments:
- tokens: bfloat16 [9728, 4096], P(('dp', 'expert'), 'etp'), may hold values from -6 to 6
- cotangent: bfloat16 [9728, 4096], P(('dp', 'expert'), 'etp'), may hold values from -6 to 6
- gates: bfloat16 [9728, 8], P(('dp', 'expert')), may hold values from 0.049804688 to 0.5
- experts_hit: int32 [9728, 8], P(('dp', 'expert')), may hold values from -1 to 15, as said below
- positions: int32 [9728, 8], P(('dp', 'expert')), may hold values from -1 to 18, as said below
- gate_w: bfloat16 [16, 4096, 1536], P('expert', 'dp', 'etp'), may hold values from -0.09375 to 0.09375
- up_w: bfloat16 [16, 4096, 1536], P('expert', 'dp', 'etp'), may hold values from -0.09375 to 0.09375
- down_w: bfloat16 [16, 1536, 4096], P('expert', 'etp', 'dp'), may hold values from -0.15625 to 0.15625
Outputs:
- input_grad: bfloat16 [9728, 4096], P(('dp', 'expert'), 'etp')
- down_grad: bfloat16 [16, 1536, 4096], P('expert', 'etp', 'dp')
Inputs may be any that keep to these rules, and one draw needn't show every extreme that they name: experts_hit and positions are -1 together, for routes to experts outside these 16. In the rows of one device, the routes to one expert hold positions 0 to n - 1 once each, with n between 1 and 19; no token names an expert twice. `positions`: see experts_hit.
All inputs are finite; a program needn't handle non-finite values.
Results may differ from a plain program's by a relative error of at most 0.018.
Values may be sent and summed in bfloat16 or wider, within the bound.
No kernel may reach another device: no remote copies, remote signals or barrier semaphores. Data moves between devices by JAX's collectives and lax.ppermute only.
A program may use at most 64 MiB of HBM per device.

v0:
```python
import jax
import jax.numpy as jnp
from jax import lax
from jax.sharding import PartitionSpec as P

CAP = 19


def expert_grads(feats, grads, gate_col, w_gate, w_up, w_down):
    gate_pre = jnp.dot(feats, w_gate, preferred_element_type=jnp.float32)
    up_pre = jnp.dot(feats, w_up, preferred_element_type=jnp.float32)
    sig = jax.nn.sigmoid(gate_pre)
    act = gate_pre * sig
    hidden_b = (act * up_pre).astype(jnp.bfloat16)
    back = lax.dot_general(
        grads, w_down, (((1,), (1,)), ((), ())), preferred_element_type=jnp.float32
    )
    gate_f = gate_col.astype(jnp.float32)[:, None]
    d_hidden = gate_f * back
    d_gate_b = (d_hidden * up_pre * sig * (1.0 + gate_pre * (1.0 - sig))).astype(jnp.bfloat16)
    d_up_b = (d_hidden * act).astype(jnp.bfloat16)
    d_part = lax.dot_general(
        d_gate_b, w_gate, (((1,), (1,)), ((), ())), preferred_element_type=jnp.float32
    )
    d_part = d_part + lax.dot_general(
        d_up_b, w_up, (((1,), (1,)), ((), ())), preferred_element_type=jnp.float32
    )
    scaled = (gate_f * grads).astype(jnp.bfloat16)
    term = lax.dot_general(
        hidden_b, scaled, (((0,), (0,)), ((), ())), preferred_element_type=jnp.float32
    )
    return (d_part.astype(jnp.bfloat16), term)


def local(tokens, cotangent, gates, experts_hit, positions, gate_w, up_w, down_w):
    width = lax.axis_size("expert")
    rows_dev = tokens.shape[0]
    routes = experts_hit.shape[1]
    slots = width * CAP
    valid = experts_hit >= 0
    flat = jnp.where(valid, experts_hit * CAP + positions, slots)
    flat_all = flat.reshape(-1)
    token_ids = jnp.repeat(jnp.arange(rows_dev, dtype=jnp.int32), routes)
    owner = jnp.zeros((slots + 1,), jnp.int32).at[flat_all].set(token_ids)[:slots]
    filled = jnp.zeros((slots + 1,), jnp.bool_).at[flat_all].set(True)[:slots]
    slot_gate = jnp.zeros((slots + 1,), jnp.bfloat16).at[flat_all].set(gates.reshape(-1))[:slots]
    slot_gate = slot_gate.reshape(width, CAP)

    def pack(source):
        rows = jnp.where(filled[:, None], source[owner], jnp.zeros((), source.dtype))
        return rows.reshape(width, CAP, source.shape[1])

    full_x, full_dy = (
        lax.all_gather(tokens, "etp", axis=1, tiled=True),
        lax.all_gather(cotangent, "etp", axis=1, tiled=True),
    )
    recv_x, recv_dy, recv_gate = (
        lax.all_to_all(pack(full_x), "expert", split_axis=0, concat_axis=0, tiled=True),
        lax.all_to_all(pack(full_dy), "expert", split_axis=0, concat_axis=0, tiled=True),
        lax.all_to_all(slot_gate, "expert", split_axis=0, concat_axis=0, tiled=True),
    )
    full_width = recv_x.shape[2]
    feats = recv_x.reshape(slots, full_width)
    grads = recv_dy.reshape(slots, full_width)
    w_gate, w_up, w_down = (
        lax.all_gather(gate_w[0], "dp", axis=0, tiled=True),
        lax.all_gather(up_w[0], "dp", axis=0, tiled=True),
        lax.all_gather(down_w[0], "dp", axis=1, tiled=True),
    )
    d_part_b, term = expert_grads(feats, grads, recv_gate.reshape(slots), w_gate, w_up, w_down)
    down_grad = lax.psum_scatter(term.astype(jnp.bfloat16), "dp", scatter_dimension=1, tiled=True)[
        None
    ]
    summed = lax.psum_scatter(
        d_part_b.astype(jnp.float32).astype(jnp.bfloat16), "etp", scatter_dimension=1, tiled=True
    ).astype(jnp.float32)
    returned = lax.all_to_all(
        summed.reshape(width, CAP, summed.shape[1]).astype(jnp.bfloat16),
        "expert",
        split_axis=0,
        concat_axis=0,
        tiled=True,
    ).astype(jnp.float32)
    narrow = returned.shape[2]
    table = jnp.concatenate(
        [returned.reshape(slots, narrow), jnp.zeros((1, narrow), jnp.float32)], axis=0
    )
    total = jnp.zeros((rows_dev, narrow), jnp.float32)
    for route in range(routes):
        total = total + table[flat[:, route]]
    input_grad = total.astype(jnp.bfloat16)
    return (input_grad, down_grad)


def solution(mesh):
    placed = (
        P(("dp", "expert"), "etp"),
        P(("dp", "expert"), "etp"),
        P(("dp", "expert"), None),
        P(("dp", "expert"), None),
        P(("dp", "expert"), None),
        P("expert", "dp", "etp"),
        P("expert", "dp", "etp"),
        P("expert", "etp", "dp"),
    )
    return jax.shard_map(
        local,
        mesh=mesh,
        in_specs=placed,
        out_specs=(P(("dp", "expert"), "etp"), P("expert", "etp", "dp")),
        check_vma=False,
    )
```

profile of v0, /device:TPU:8, one launch (start us, length us, event | category | flops | bytes accessed | tf_op | source)
XLA Modules:
  0.0 373.5 jit_solution(14487152539822425806)
XLA Ops:
  11.4 12.6 %scatter_custom_fusion = bf16[305]{0:T(512)(128)(2,1)S(1)} fusion(s32[1216]{0:T(1024)S(1)} %fusion.18, bf16[1216]{0:T(1024)(128)(2,1)S(1)} %reshape.171, bf16[]{:T(256)} %constant.9.clone.1), kind=kCustom, calls=%fused_computation.64 | custom fusion | bytes 612 | tf_op jit(solution)/shard_map/scatter | solution.py:46
  24.7 10.4 %all-to-all-start = ((bf16[16,1,19]{2,1,0:T(2,128)(2,1)}), bf16[16,1,19]{2,1,0:T(2,128)(2,1)S(1)}, u32[]{:S(2)}, u32[]{:S(2)}) async-start(bf16[16,1,19]{2,1,0:T(2,128)(2,1)} %all_to_all.20), calls=%async_computation | async-start | bytes 16384 | tf_op jit(solution)/shard_map/all_to_all | solution.py:60
  35.3 11.4 %scatter_custom_fusion.1 = pred[305]{0:T(512)(128)(4,1)S(1)} fusion(s32[1216]{0:T(1024)S(1)} %fusion.18, pred[1216]{0:T(1024)(128)(4,1)S(1)} %broadcast.66, pred[]{:T(512)} %constant.14.clone.1), kind=kCustom, calls=%fused_computation.62 | custom fusion | bytes 306 | tf_op jit(solution)/shard_map/scatter | solution.py:45
  46.8 6.4 %scatter_custom_fusion.2 = s32[305]{0:T(512)S(1)} fusion(s32[1216]{0:T(1024)S(1)} %fusion.18, s32[1216]{0:T(1024)S(1)} %reshape.187, s32[]{:T(128)} %constant.10.clone.1), kind=kCustom, calls=%fused_computation.60 | custom fusion | bytes 1224 | tf_op jit(solution)/shard_map/scatter | solution.py:44
  53.2 3.7 all-gather.9.cloned.1.call-done
  56.9 9.5 %gather_fusion = bf16[304,4096]{1,0:T(8,128)(2,1)} fusion(bf16[152,4096]{1,0:T(8,128)(2,1)} %all-gather.9.cloned.1.call-done, s32[1024]{0:T(1024)S(1)} %pad_clamp_fusion.8), kind=kCustom, calls=%fused_computation | custom fusion | bytes 4981952 | tf_op jit(solution)/shard_map/gather | solution.py:50
  68.5 30.9 %all-gather.11.cloned.1.call-done = bf16[152,4096]{1,0:T(8,128)(2,1)} async-done(((bf16[152,512]{1,0:T(8,128)(2,1)}), bf16[152,4096]{1,0:T(8,128)(2,1)}) %all-gather.11.cloned.1.call-update) | async-done | bytes 1245200 | tf_op jit(solution)/shard_map/all_gather | solution.py:54
  99.4 9.5 %gather_fusion.1 = bf16[304,4096]{1,0:T(8,128)(2,1)} fusion(bf16[152,4096]{1,0:T(8,128)(2,1)} %all-gather.11.cloned.1.call-done, s32[1024]{0:T(1024)S(1)} %pad_clamp_fusion.8), kind=kCustom, calls=%fused_computation.1 | custom fusion | bytes 4981952 | tf_op jit(solution)/shard_map/gather | solution.py:50
  108.9 3.4 gather.37
  112.3 5.0 %broadcast_select_fusion.1 = (bf16[16,19,4096]{2,1,0:T(8,128)(2,1)}, bf16[16,19,4096]{2,1,0:T(8,128)(2,1)}) fusion(bf16[16,19,4096]{2,1,0:T(8,128)(2,1)S(1)} %gather.35, pred[16,19]{1,0:T(8,128)(4,1)S(1)} %broadcast_in_dim.63, bf16[16,19,4096]{2,1,0:T(8,128)(2,1)} %gather.37), kind=kLoop, calls=%fused_computation.18 | loop fusion | flops 2490368 | bytes 9961776 | tf_op jit(solution)/shard_map/jit(_where)/select_n | solution.py:50
  117.3 7.5 %all-to-all-start.1 = ((bf16[16,19,4096]{2,1,0:T(8,128)(2,1)}), bf16[16,19,4096]{2,1,0:T(8,128)(2,1)S(1)}, u32[]{:S(2)}, u32[]{:S(2)}) async-start(bf16[16,19,4096]{2,1,0:T(8,128)(2,1)} %get-tuple-element.10), calls=%async_computation.1 | async-start | bytes 6291456 | tf_op jit(solution)/shard_map/all_to_all | solution.py:59
  125.3 71.2 %all-to-all-done.1 = bf16[16,19,4096]{2,1,0:T(8,128)(2,1)S(1)} async-done(((bf16[16,19,4096]{2,1,0:T(8,128)(2,1)}), bf16[16,19,4096]{2,1,0:T(8,128)(2,1)S(1)}, u32[]{:S(2)}, u32[]{:S(2)}) %all-to-all-start.1) | async-done | bytes 2490400 | tf_op jit(solution)/shard_map/all_to_all | solution.py:59
  196.5 4.7 %all-to-all-start.2 = ((bf16[16,19,4096]{2,1,0:T(8,128)(2,1)}), bf16[16,19,4096]{2,1,0:T(8,128)(2,1)}, u32[]{:S(2)}, u32[]{:S(2)}) async-start(bf16[16,19,4096]{2,1,0:T(8,128)(2,1)} %get-tuple-element.11), calls=%async_computation.2 | async-start | bytes 6291456 | tf_op jit(solution)/shard_map/all_to_all | solution.py:58
  204.8 68.2 %all-to-all-done.2 = bf16[16,19,4096]{2,1,0:T(8,128)(2,1)} async-done(((bf16[16,19,4096]{2,1,0:T(8,128)(2,1)}), bf16[16,19,4096]{2,1,0:T(8,128)(2,1)}, u32[]{:S(2)}, u32[]{:S(2)}) %all-to-all-start.2) | async-done | bytes 2490400 | tf_op jit(solution)/shard_map/all_to_all | solution.py:58
  273.0 2.3 reshape.84
  276.8 2.6 fusion.4
  279.5 3.5 fusion.7
  283.0 2.7 fusion.11
  287.2 2.3 fusion
  289.6 2.2 convolution_convert_fusion
  291.9 39.0 %reduce-scatter.3.cloned.1.call-done = bf16[304,512]{1,0:T(8,128)(2,1)} async-done(((bf16[304,4096]{1,0:T(8,128)(2,1)}), bf16[304,512]{1,0:T(8,128)(2,1)}) %reduce-scatter.3.cloned.1.call-update) | async-done | bytes 311312 | tf_op jit(solution)/shard_map/reduce_scatter | solution.py:74
  332.7 7.5 %all-to-all-start.3 = ((bf16[16,19,512]{2,1,0:T(8,128)(2,1)}), bf16[16,19,512]{2,1,0:T(8,128)(2,1)S(1)}, u32[]{:S(2)}, u32[]{:S(2)}) async-start(bf16[16,19,512]{2,1,0:T(8,128)(2,1)} %convert_element_type.47), calls=%async_computation.4 | async-start | bytes 786432 | tf_op jit(solution)/shard_map/all_to_all | solution.py:77
  340.3 13.6 %all-to-all-done.3 = bf16[16,19,512]{2,1,0:T(8,128)(2,1)S(1)} async-done(((bf16[16,19,512]{2,1,0:T(8,128)(2,1)}), bf16[16,19,512]{2,1,0:T(8,128)(2,1)S(1)}, u32[]{:S(2)}, u32[]{:S(2)}) %all-to-all-start.3) | async-done | bytes 311328 | tf_op jit(solution)/shard_map/all_to_all | solution.py:77
  361.4 4.8 %reduce-scatter.5.cloned.1.call-done = bf16[192,1024]{1,0:T(8,128)(2,1)} async-done(((bf16[192,4096]{1,0:T(8,128)(2,1)}), bf16[192,1024]{1,0:T(8,128)(2,1)}) %reduce-scatter.5.cloned.1.call-update) | async-done | bytes 393232 | tf_op jit(solution)/shard_map/reduce_scatter | solution.py:71
  (65 shorter events, 22.9 us)
Async XLA Ops:
  8.0 48.9 %all-gather.9.cloned.1.call-start = ((), (), s32[]{:S(2)}) async-start(), calls=%async_computation.6 | async-start | bytes 1400832 | tf_op jit(solution)/shard_map/all_gather | solution.py:55
  8.7 90.7 %all-gather.11.cloned.1.call-start = ((), (), s32[]{:S(2)}) async-start(), calls=%async_computation.7 | async-start | bytes 1400832 | tf_op jit(solution)/shard_map/all_gather | solution.py:54
  24.7 92.5 %all-to-all-start = ((bf16[16,1,19]{2,1,0:T(2,128)(2,1)}), bf16[16,1,19]{2,1,0:T(2,128)(2,1)S(1)}, u32[]{:S(2)}, u32[]{:S(2)}) async-start(bf16[16,1,19]{2,1,0:T(2,128)(2,1)} %all_to_all.20), calls=%async_computation | async-start | bytes 16384 | tf_op jit(solution)/shard_map/all_to_all | solution.py:60
  117.3 79.2 %all-to-all-start.1 = ((bf16[16,19,4096]{2,1,0:T(8,128)(2,1)}), bf16[16,19,4096]{2,1,0:T(8,128)(2,1)S(1)}, u32[]{:S(2)}, u32[]{:S(2)}) async-start(bf16[16,19,4096]{2,1,0:T(8,128)(2,1)} %get-tuple-element.10), calls=%async_computation.1 | async-start | bytes 6291456 | tf_op jit(solution)/shard_map/all_to_all | solution.py:59
  124.7 150.7 %all-gather.17.cloned.1.call-start = ((), (), s32[]{:S(2)}) async-start(), calls=%async_computation.12 | async-start | bytes 1966080 | tf_op jit(solution)/shard_map/all_gather | solution.py:66
  196.5 76.5 %all-to-all-start.2 = ((bf16[16,19,4096]{2,1,0:T(8,128)(2,1)}), bf16[16,19,4096]{2,1,0:T(8,128)(2,1)}, u32[]{:S(2)}, u32[]{:S(2)}) async-start(bf16[16,19,4096]{2,1,0:T(8,128)(2,1)} %get-tuple-element.11), calls=%async_computation.2 | async-start | bytes 6291456 | tf_op jit(solution)/shard_map/all_to_all | solution.py:58
  201.2 78.3 %all-gather.15.cloned.1.call-start = ((), (), s32[]{:S(2)}) async-start(), calls=%async_computation.11 | async-start | bytes 1966080 | tf_op jit(solution)/shard_map/all_gather | solution.py:67
  201.8 81.2 %all-gather.13.cloned.1.call-start = ((), (), s32[]{:S(2)}) async-start(), calls=%async_computation.10 | async-start | bytes 1966080 | tf_op jit(solution)/shard_map/all_gather | solution.py:68
  202.4 128.5 %reduce-scatter.3.cloned.1.call-start = ((), (), s32[]{:S(2)}) async-start(), calls=%async_computation.8 | async-start | bytes 2801664 | tf_op jit(solution)/shard_map/reduce_scatter | solution.py:74
  275.4 1.5 copy-start.1
  279.4 3.6 copy-start
  283.0 2.7 copy-start.3
  285.8 1.4 copy-start.2
  289.5 76.7 %reduce-scatter.5.cloned.1.call-start = ((), (), s32[]{:S(2)}) async-start(), calls=%async_computation.9 | async-start | bytes 1966080 | tf_op jit(solution)/shard_map/reduce_scatter | solution.py:71
  332.7 21.2 %all-to-all-start.3 = ((bf16[16,19,512]{2,1,0:T(8,128)(2,1)}), bf16[16,19,512]{2,1,0:T(8,128)(2,1)S(1)}, u32[]{:S(2)}, u32[]{:S(2)}) async-start(bf16[16,19,512]{2,1,0:T(8,128)(2,1)} %convert_element_type.47), calls=%async_computation.4 | async-start | bytes 786432 | tf_op jit(solution)/shard_map/all_to_all | solution.py:77
Sparse Core Ops, SparseCore 0:
  10.9 45.9 all-gather.8
  59.0 40.4 all-gather.10
  289.7 41.1 reduce-scatter.2
  334.4 31.7 reduce-scatter.4
Sparse Core Ops, SparseCore 1:
  127.3 30.4 all-gather.16
  203.8 30.4 all-gather.14
  236.2 31.8 all-gather.12
where the time goes:
time: 374 us
  waiting for transfers between devices  234 us (63%)
  local copies, waits for them, and re-layouts  71.7 us (19%)
  starting transfers between devices  30.6 us (8%)
  between operations  15.8 us (4%)
  matrix products  14.3 us (4%)
  other arithmetic  6.76 us (2%)
    all_to_all x1, waiting for transfers between devices, local(): lax.all_to_all(pack(full_dy), 'expert', split_axis=0, concat_axis=0, tile...  71.2 us
    all_to_all x1, waiting for transfers between devices, local(): lax.all_to_all(pack(full_x), 'expert', split_axis=0, concat_axis=0, tiled...  68.2 us
    reduce_scatter x1, waiting for transfers between devices, local(): lax.psum_scatter(d_part_b.astype(jnp.float32).astype(jnp.bfloat16), 'etp'...  39 us
    all_gather x1, waiting for transfers between devices, local(): lax.all_gather(tokens, 'etp', axis=1, tiled=True)  30.9 us
    gather x4, local copies, waits for them, and re-layouts, pack(): source[owner]  24.5 us
    all_to_all x1, waiting for transfers between devices, local(): lax.all_to_all(summed.reshape(width, CAP, summed.shape[1]).astype(jnp.bfl...  13.6 us
    scatter x1, local copies, waits for them, and re-layouts, local(): jnp.zeros((slots + 1,), jnp.bfloat16).at[flat_all].set(gates.reshape(-1))  12.6 us
    scatter x1, local copies, waits for them, and re-layouts, local(): filled = jnp.zeros((slots + 1,), jnp.bool_).at[flat_all].set(True)[:slots]  11.4 us
  transfers between devices with their start and end apart: 11, of which 7 were waited for; matrix products, arithmetic and copies ran while one was open for 23% of the time, Pallas kernels for 0%

commit v1 on v0

--- a/solution.py
+++ b/solution.py
@@ -4,6 +4,12 @@
 from jax.sharding import PartitionSpec as P
 
 CAP = 19
+
+
+def tiled_gather(x, axis, dim):
+    size = lax.axis_size(axis)
+    repeats = [size if d == dim else 1 for d in range(x.ndim)]
+    return lax.all_to_all(jnp.tile(x, repeats), axis, split_axis=dim, concat_axis=dim, tiled=True)
 
 
 def expert_grads(feats, grads, gate_col, w_gate, w_up, w_down):
@@ -51,7 +57,7 @@
         return rows.reshape(width, CAP, source.shape[1])
 
     full_x, full_dy = (
-        lax.all_gather(tokens, "etp", axis=1, tiled=True),
+        tiled_gather(tokens, "etp", 1),
         lax.all_gather(cotangent, "etp", axis=1, tiled=True),
     )
     recv_x, recv_dy, recv_gate = (

time: 374 us -> 346 us (0.925)
  waiting for transfers between devices: 234 us -> 201 us
  starting transfers between devices: 30.6 us -> 40.5 us
  local copies, waits for them, and re-layouts: 71.7 us -> 67.6 us
    all_gather x1 -> x0, waiting for transfers between devices: 30.9 us -> none  [local(): lax.all_gather(tokens, 'etp', axis=1, tiled=True)]
    all_to_all x0 -> x1, starting transfers between devices: none -> 9.29 us  [tiled_gather(): lax.all_to_all(jnp.tile(x, repeats), axis, split_axis=dim, concat_axis=di...]
    gather x4, local copies, waits for them, and re-layouts: 24.5 us -> 18.8 us  [pack(): source[owner]]
  transfers between devices with their start and end apart: 11 -> 11, of which waited for: 7 -> 6; matrix products, arithmetic and copies ran while one was open for 23% -> 22% of each run, Pallas kernels for 0% -> 0%
where the time goes in v1:
time: 346 us; the launch traced here: 345 us
  waiting for transfers between devices  201 us (58%)
  local copies, waits for them, and re-layouts  67.6 us (20%)
  starting transfers between devices  40.5 us (12%)
  between operations  15.9 us (5%)
  matrix products  14.3 us (4%)
  other arithmetic  6.03 us (2%)
    all_to_all x1, waiting for transfers between devices, local(): lax.all_to_all(pack(full_dy), 'expert', split_axis=0, concat_axis=0, tile...  71.2 us
    all_to_all x1, waiting for transfers between devices, local(): lax.all_to_all(pack(full_x), 'expert', split_axis=0, concat_axis=0, tiled...  68.2 us
    reduce_scatter x1, waiting for transfers between devices, local(): lax.psum_scatter(d_part_b.astype(jnp.float32).astype(jnp.bfloat16), 'etp'...  40.7 us
    gather x4, local copies, waits for them, and re-layouts, pack(): source[owner]  18.8 us
    all_to_all x1, waiting for transfers between devices, local(): lax.all_to_all(summed.reshape(width, CAP, summed.shape[1]).astype(jnp.bfl...  13.6 us
    scatter x1, local copies, waits for them, and re-layouts, local(): jnp.zeros((slots + 1,), jnp.bfloat16).at[flat_all].set(gates.reshape(-1))  12.8 us
    all_to_all x1, starting transfers between devices, local(): lax.all_to_all(slot_gate, 'expert', split_axis=0, concat_axis=0, tiled=True)  11.5 us
    scatter x1, local copies, waits for them, and re-layouts, local(): filled = jnp.zeros((slots + 1,), jnp.bool_).at[flat_all].set(True)[:slots]  11.2 us
  transfers between devices with their start and end apart: 11, of which 6 were waited for; matrix products, arithmetic and copies ran while one was open for 22% of the time, Pallas kernels for 0%

profile of v1, /device:TPU:8, one launch (start us, length us, event | category | flops | bytes accessed | tf_op | source)
XLA Modules:
  0.0 345.5 jit_solution(9665939813137873433)
XLA Ops:
  10.1 9.3 %all-to-all-start.2 = ((bf16[152,8,512]{2,0,1:T(8,128)(2,1)}), bf16[152,8,512]{2,0,1:T(8,128)(2,1)S(1)}, u32[]{:S(2)}, u32[]{:S(2)}) async-start(bf16[152,8,512]{2,0,1:T(8,128)(2,1)} %tile.2), calls=%async_computation.2 | async-start | bytes 2490368 | tf_op jit(solution)/shard_map/all_to_all | solution.py:12
  20.5 11.2 %scatter_custom_fusion.1 = pred[305]{0:T(512)(128)(4,1)S(1)} fusion(s32[1216]{0:T(1024)S(1)} %fusion.18, pred[1216]{0:T(1024)(128)(4,1)S(1)} %broadcast.69, pred[]{:T(512)} %constant.14.clone.1), kind=kCustom, calls=%fused_computation.62 | custom fusion | bytes 306 | tf_op jit(solution)/shard_map/scatter | solution.py:51
  32.1 12.8 %scatter_custom_fusion = bf16[305]{0:T(512)(128)(2,1)S(1)} fusion(s32[1216]{0:T(1024)S(1)} %fusion.18, bf16[1216]{0:T(1024)(128)(2,1)S(1)} %reshape.178, bf16[]{:T(256)} %constant.9.clone.1), kind=kCustom, calls=%fused_computation.64 | custom fusion | bytes 612 | tf_op jit(solution)/shard_map/scatter | solution.py:52
  45.6 6.4 %scatter_custom_fusion.2 = s32[305]{0:T(512)S(1)} fusion(s32[1216]{0:T(1024)S(1)} %fusion.18, s32[1216]{0:T(1024)S(1)} %reshape.194, s32[]{:T(128)} %constant.10.clone.1), kind=kCustom, calls=%fused_computation.60 | custom fusion | bytes 1224 | tf_op jit(solution)/shard_map/scatter | solution.py:50
  52.8 11.5 %all-to-all-start = ((bf16[16,1,19]{2,1,0:T(2,128)(2,1)}), bf16[16,1,19]{2,1,0:T(2,128)(2,1)S(1)}, u32[]{:S(2)}, u32[]{:S(2)}) async-start(bf16[16,1,19]{2,1,0:T(2,128)(2,1)} %all_to_all.28), calls=%async_computation | async-start | bytes 16384 | tf_op jit(solution)/shard_map/all_to_all | solution.py:66
  64.5 3.8 %gather_fusion.1 = bf16[304,4096]{1,0:T(8,128)(2,1)} fusion(bf16[152,4096]{1,0:T(8,128)(2,1)S(1)} %bitcast.31, s32[1024]{0:T(1024)S(1)} %pad_clamp_fusion.8), kind=kCustom, calls=%fused_computation.1 | custom fusion | bytes 4981952 | tf_op jit(solution)/shard_map/gather | solution.py:56
  68.3 2.2 gather.37
  70.5 9.5 %gather_fusion = bf16[304,4096]{1,0:T(8,128)(2,1)} fusion(bf16[152,4096]{1,0:T(8,128)(2,1)} %all-gather.8.cloned.1.call-done, s32[1024]{0:T(1024)S(1)} %pad_clamp_fusion.8), kind=kCustom, calls=%fused_computation | custom fusion | bytes 4981952 | tf_op jit(solution)/shard_map/gather | solution.py:56
  79.9 3.4 gather.35
  83.3 5.0 %broadcast_select_fusion.1 = (bf16[16,19,4096]{2,1,0:T(8,128)(2,1)}, bf16[16,19,4096]{2,1,0:T(8,128)(2,1)}) fusion(bf16[16,19,4096]{2,1,0:T(8,128)(2,1)} %gather.35, pred[16,19]{1,0:T(8,128)(4,1)S(1)} %broadcast_in_dim.63, bf16[16,19,4096]{2,1,0:T(8,128)(2,1)S(1)} %gather.37), kind=kLoop, calls=%fused_computation.18 | loop fusion | flops 2490368 | bytes 9961776 | tf_op jit(solution)/shard_map/jit(_where)/select_n | solution.py:56
  88.3 7.3 %all-to-all-start.1 = ((bf16[16,19,4096]{2,1,0:T(8,128)(2,1)}), bf16[16,19,4096]{2,1,0:T(8,128)(2,1)S(1)}, u32[]{:S(2)}, u32[]{:S(2)}) async-start(bf16[16,19,4096]{2,1,0:T(8,128)(2,1)} %get-tuple-element.10), calls=%async_computation.1 | async-start | bytes 6291456 | tf_op jit(solution)/shard_map/all_to_all | solution.py:65
  96.2 71.2 %all-to-all-done.1 = bf16[16,19,4096]{2,1,0:T(8,128)(2,1)S(1)} async-done(((bf16[16,19,4096]{2,1,0:T(8,128)(2,1)}), bf16[16,19,4096]{2,1,0:T(8,128)(2,1)S(1)}, u32[]{:S(2)}, u32[]{:S(2)}) %all-to-all-start.1) | async-done | bytes 2490400 | tf_op jit(solution)/shard_map/all_to_all | solution.py:65
  167.4 4.7 %all-to-all-start.3 = ((bf16[16,19,4096]{2,1,0:T(8,128)(2,1)}), bf16[16,19,4096]{2,1,0:T(8,128)(2,1)}, u32[]{:S(2)}, u32[]{:S(2)}) async-start(bf16[16,19,4096]{2,1,0:T(8,128)(2,1)} %get-tuple-element.11), calls=%async_computation.3 | async-start | bytes 6291456 | tf_op jit(solution)/shard_map/all_to_all | solution.py:64
  175.7 68.2 %all-to-all-done.3 = bf16[16,19,4096]{2,1,0:T(8,128)(2,1)} async-done(((bf16[16,19,4096]{2,1,0:T(8,128)(2,1)}), bf16[16,19,4096]{2,1,0:T(8,128)(2,1)}, u32[]{:S(2)}, u32[]{:S(2)}) %all-to-all-start.3) | async-done | bytes 2490400 | tf_op jit(solution)/shard_map/all_to_all | solution.py:64
  243.9 2.3 reshape.91
  247.7 2.6 fusion.4
  250.4 3.5 %fusion.7 = f32[304,192]{0,1:T(8,128)S(1)} fusion(bf16[304,4096]{1,0:T(8,128)(2,1)} %copy-done.1, bf16[1,4096,192]{1,2,0:T(8,128)(2,1)} %all-gather.12.cloned.1.call-done), kind=kOutput, calls=%fused_computation.25 | convolution fusion | flops 478150656 | bytes 4296704 | tf_op jit(solution)/shard_map/dot_general | solution.py:17
  253.9 2.7 fusion.11
  258.0 2.4 fusion
  260.5 2.3 convolution_convert_fusion
  262.8 40.7 %reduce-scatter.3.cloned.1.call-done = bf16[304,512]{1,0:T(8,128)(2,1)} async-done(((bf16[304,4096]{1,0:T(8,128)(2,1)}), bf16[304,512]{1,0:T(8,128)(2,1)}) %reduce-scatter.3.cloned.1.call-update) | async-done | bytes 311312 | tf_op jit(solution)/shard_map/reduce_scatter | solution.py:80
  305.3 7.3 %all-to-all-start.4 = ((bf16[16,19,512]{2,1,0:T(8,128)(2,1)}), bf16[16,19,512]{2,1,0:T(8,128)(2,1)S(1)}, u32[]{:S(2)}, u32[]{:S(2)}) async-start(bf16[16,19,512]{2,1,0:T(8,128)(2,1)} %convert_element_type.47), calls=%async_computation.5 | async-start | bytes 786432 | tf_op jit(solution)/shard_map/all_to_all | solution.py:83
  312.7 13.6 %all-to-all-done.4 = bf16[16,19,512]{2,1,0:T(8,128)(2,1)S(1)} async-done(((bf16[16,19,512]{2,1,0:T(8,128)(2,1)}), bf16[16,19,512]{2,1,0:T(8,128)(2,1)S(1)}, u32[]{:S(2)}, u32[]{:S(2)}) %all-to-all-start.4) | async-done | bytes 311328 | tf_op jit(solution)/shard_map/all_to_all | solution.py:83
  333.8 4.3 %reduce-scatter.5.cloned.1.call-done = bf16[192,1024]{1,0:T(8,128)(2,1)} async-done(((bf16[192,4096]{1,0:T(8,128)(2,1)}), bf16[192,1024]{1,0:T(8,128)(2,1)}) %reduce-scatter.5.cloned.1.call-update) | async-done | bytes 393232 | tf_op jit(solution)/shard_map/reduce_scatter | solution.py:77
  (72 shorter events, 21.6 us)
Async XLA Ops:
  8.0 12.1 %copy-start.5 = (s32[152,8]{0,1:T(8,128)S(1)}, s32[152,8]{0,1:T(8,128)}, u32[]{:S(2)}) copy-start(s32[152,8]{0,1:T(8,128)} %param.11) | copy-start | bytes 14596
  8.0 12.1 %copy-start.4 = (s32[152,8]{0,1:T(8,128)S(1)}, s32[152,8]{0,1:T(8,128)}, u32[]{:S(2)}) copy-start(s32[152,8]{0,1:T(8,128)} %param.12) | copy-start | bytes 14596
  8.0 23.8 %copy-start.6 = (bf16[152,8]{0,1:T(8,128)(2,1)S(1)}, bf16[152,8]{0,1:T(8,128)(2,1)}, u32[]{:S(2)}) copy-start(bf16[152,8]{0,1:T(8,128)(2,1)} %param.10) | copy-start | bytes 7300
  10.1 42.8 %all-to-all-start.2 = ((bf16[152,8,512]{2,0,1:T(8,128)(2,1)}), bf16[152,8,512]{2,0,1:T(8,128)(2,1)S(1)}, u32[]{:S(2)}, u32[]{:S(2)}) async-start(bf16[152,8,512]{2,0,1:T(8,128)(2,1)} %tile.2), calls=%async_computation.2 | async-start | bytes 2490368 | tf_op jit(solution)/shard_map/all_to_all | solution.py:12
  19.4 51.1 %all-gather.8.cloned.1.call-start = ((), (), s32[]{:S(2)}) async-start(), calls=%async_computation.7 | async-start | bytes 1400832 | tf_op jit(solution)/shard_map/all_gather | solution.py:61
  52.8 35.4 %all-to-all-start = ((bf16[16,1,19]{2,1,0:T(2,128)(2,1)}), bf16[16,1,19]{2,1,0:T(2,128)(2,1)S(1)}, u32[]{:S(2)}, u32[]{:S(2)}) async-start(bf16[16,1,19]{2,1,0:T(2,128)(2,1)} %all_to_all.28), calls=%async_computation | async-start | bytes 16384 | tf_op jit(solution)/shard_map/all_to_all | solution.py:66
  88.3 79.1 %all-to-all-start.1 = ((bf16[16,19,4096]{2,1,0:T(8,128)(2,1)}), bf16[16,19,4096]{2,1,0:T(8,128)(2,1)S(1)}, u32[]{:S(2)}, u32[]{:S(2)}) async-start(bf16[16,19,4096]{2,1,0:T(8,128)(2,1)} %get-tuple-element.10), calls=%async_computation.1 | async-start | bytes 6291456 | tf_op jit(solution)/shard_map/all_to_all | solution.py:65
  95.6 150.7 %all-gather.14.cloned.1.call-start = ((), (), s32[]{:S(2)}) async-start(), calls=%async_computation.12 | async-start | bytes 1966080 | tf_op jit(solution)/shard_map/all_gather | solution.py:72
  167.4 76.5 %all-to-all-start.3 = ((bf16[16,19,4096]{2,1,0:T(8,128)(2,1)}), bf16[16,19,4096]{2,1,0:T(8,128)(2,1)}, u32[]{:S(2)}, u32[]{:S(2)}) async-start(bf16[16,19,4096]{2,1,0:T(8,128)(2,1)} %get-tuple-element.11), calls=%async_computation.3 | async-start | bytes 6291456 | tf_op jit(solution)/shard_map/all_to_all | solution.py:64
  172.1 78.3 %all-gather.12.cloned.1.call-start = ((), (), s32[]{:S(2)}) async-start(), calls=%async_computation.11 | async-start | bytes 1966080 | tf_op jit(solution)/shard_map/all_gather | solution.py:73
  172.7 81.2 %all-gather.10.cloned.1.call-start = ((), (), s32[]{:S(2)}) async-start(), calls=%async_computation.10 | async-start | bytes 1966080 | tf_op jit(solution)/shard_map/all_gather | solution.py:74
  173.3 130.2 %reduce-scatter.3.cloned.1.call-start = ((), (), s32[]{:S(2)}) async-start(), calls=%async_computation.8 | async-start | bytes 2801664 | tf_op jit(solution)/shard_map/reduce_scatter | solution.py:80
  246.2 1.5 copy-start.1
  250.3 3.6 %copy-start = (bf16[304,4096]{1,0:T(8,128)(2,1)S(1)}, bf16[304,4096]{1,0:T(8,128)(2,1)}, u32[]{:S(2)}) copy-start(bf16[304,4096]{1,0:T(8,128)(2,1)} %reshape.90) | copy-start | bytes 7471108
  253.9 2.7 copy-start.3
  256.6 1.4 copy-start.2
  260.4 77.7 %reduce-scatter.5.cloned.1.call-start = ((), (), s32[]{:S(2)}) async-start(), calls=%async_computation.9 | async-start | bytes 1966080 | tf_op jit(solution)/shard_map/reduce_scatter | solution.py:77
  305.3 21.0 %all-to-all-start.4 = ((bf16[16,19,512]{2,1,0:T(8,128)(2,1)}), bf16[16,19,512]{2,1,0:T(8,128)(2,1)S(1)}, u32[]{:S(2)}, u32[]{:S(2)}) async-start(bf16[16,19,512]{2,1,0:T(8,128)(2,1)} %convert_element_type.47), calls=%async_computation.5 | async-start | bytes 786432 | tf_op jit(solution)/shard_map/all_to_all | solution.py:83
Sparse Core Ops, SparseCore 0:
  22.3 45.9 all-gather.7
  260.5 42.8 reduce-scatter.2
  307.2 30.9 reduce-scatter.4
Sparse Core Ops, SparseCore 1:
  98.2 31.4 all-gather.13
  174.7 31.3 all-gather.11
  208.0 31.8 all-gather.9
